TPU v7x, 512 devices: a whole 4x4x16 slice. The times are simulated.
512 devices in a mesh: seq: 64 (over z, y), tp: 8 (over x, core).
Axes of the slice: x: 4, y: 4, z: 16, core: 2. Of those that a mesh axis runs over, the one named last changes fastest.
Arguments:
- residual: bfloat16 [8192, 8192], P('seq', 'tp'), may hold values from -6 to 6
- steer_table: bfloat16 [7, 8192], P(None, 'tp'), may hold values from -6 to 6
- steer_index: int32 [4], replicated, may hold values from 0 to 6
- steer_num: int32 [4], replicated, may hold values from -8 to 8
- lengths: int32 [4], replicated, may hold values from 1 to 4096, 8192 in all
- queries: bfloat16 [8192, 64, 128], P('seq', 'tp'), may hold values from -128 to 128
- keys: bfloat16 [8192, 8, 128], P('seq', 'tp'), may hold values from -6 to 6
- values: bfloat16 [8192, 8, 128], P('seq', 'tp'), may hold values from -6 to 6
- inner_x: bfloat16 [8192, 16384], P('seq', 'tp'), may hold values from -6 to 6
- dt_raw: bfloat16 [8192, 16384], P('seq', 'tp'), may hold values from -4 to 4
- dt_bias: float32 [16384], P('tp'), may hold values from -7 to -2.5
- a_log: float32 [16, 16384], P(None, 'tp'), may hold values from -2.3 to 2.77
- skip_gain: float32 [16384], P('tp'), may hold values from 0.5 to 1.5
- bc_weight: bfloat16 [32, 16384], P(None, 'tp'), may hold values from -0.046875 to 0.046875
Outputs:
- steered: bfloat16 [8192, 8192], P('seq', 'tp')
- context: bfloat16 [8192, 64, 128], P('seq', 'tp')
- mixed: bfloat16 [8192, 16384], P('seq', 'tp')
Inputs may be any that keep to these rules, and one draw needn't show every extreme that they name: `lengths`: the 4 requests lie end to end in token order and the longest has exactly 8192 // 2 tokens. `steer_num`: a request's steering multiplier is its numerator over 4.
All inputs are finite; a program needn't handle non-finite values.
Results may differ from a plain program's by a relative error of at most 0.0039.
Values may be sent and summed in bfloat16 or wider, within the bound.
A program may use at most 128 MiB of HBM per device.

v0:
```python
import jax
import jax.numpy as jnp
from jax import lax
from jax.sharding import PartitionSpec as P

NEG_FILL = -1e30
KEY_BLOCK = 512


def prefix(part, axis, combine, identity):
    place = lax.axis_index(axis)
    gathered = jax.tree.map(lambda a: lax.all_gather(a, axis), part)
    state = jax.tree.map(lambda a, e: jnp.zeros_like(a) + jnp.asarray(e, a.dtype), part, identity)

    def one(lap, state):
        return combine(
            state, jax.tree.map(lambda a: lax.dynamic_index_in_dim(a, lap, 0, False), gathered)
        )

    return lax.fori_loop(0, place, one, state)


def request_bounds(lengths, positions):
    seg_ends = jnp.cumsum(lengths)
    seg_starts = seg_ends - lengths
    member = (positions[:, None] >= seg_starts[None, :]) & (positions[:, None] < seg_ends[None, :])
    member_int = member.astype(jnp.int32)
    req_start = jnp.sum(member_int * seg_starts[None, :], axis=1)
    return (member_int, req_start)


def chain_combine(earlier, later):
    return (earlier[0] * later[0], later[0] * earlier[1] + later[1])


def shards(
    residual,
    steer_table,
    steer_index,
    steer_num,
    lengths,
    queries,
    keys,
    values,
    inner_x,
    dt_raw,
    dt_bias,
    a_log,
    skip_gain,
    bc_weight,
):
    tok_rows = residual.shape[0]
    positions = lax.axis_index("seq") * tok_rows + jnp.arange(tok_rows, dtype=jnp.int32)
    member_int, req_start = request_bounds(lengths, positions)
    vector_pick = (
        steer_index[:, None] == jnp.arange(steer_table.shape[0], dtype=jnp.int32)[None, :]
    ).astype(jnp.float32)
    vector_pick = vector_pick * (steer_num.astype(jnp.float32) * 0.25)[:, None]
    token_pick = jnp.dot(
        member_int.astype(jnp.float32), vector_pick, precision=lax.Precision.HIGHEST
    )
    steer_add = jnp.dot(
        token_pick, steer_table.astype(jnp.float32), precision=lax.Precision.HIGHEST
    )
    steered = (residual.astype(jnp.float32) + steer_add).astype(jnp.bfloat16)
    local_heads = queries.shape[1]
    local_kv = keys.shape[1]
    head_dim = queries.shape[2]
    head_group = local_heads // local_kv
    score_scale = 1.0 / head_dim**0.5
    grouped_q = queries.reshape(tok_rows, local_kv, head_group, head_dim)

    def update(carried, key_part, value_part, key_start):
        run_max, run_total, run_acc = carried
        count = key_part.shape[0]
        scores = (
            jnp.einsum("tkgd,skd->tkgs", grouped_q, key_part, preferred_element_type=jnp.float32)
            * score_scale
        )
        key_pos = key_start + jnp.arange(count, dtype=jnp.int32)
        allowed = (key_pos[None, :] <= positions[:, None]) & (
            key_pos[None, :] >= req_start[:, None]
        )
        allowed = allowed[:, None, None, :]
        masked = jnp.where(allowed, scores, NEG_FILL)
        new_max = jnp.maximum(run_max, jnp.max(masked, axis=-1))
        expo = jnp.where(allowed, jnp.exp(masked - new_max[..., None]), 0.0)
        rescale = jnp.exp(run_max - new_max)
        weights = expo.astype(jnp.bfloat16)
        run_total = run_total * rescale + jnp.sum(expo, axis=-1)
        products = jnp.einsum(
            "tkgs,skd->tkgd", weights, value_part, preferred_element_type=jnp.float32
        )
        run_acc = run_acc * rescale[..., None] + products
        return (new_max, run_total, run_acc)

    start_state = (
        jnp.full((tok_rows, local_kv, head_group), NEG_FILL, jnp.float32),
        jnp.zeros((tok_rows, local_kv, head_group), jnp.float32),
        jnp.zeros((tok_rows, local_kv, head_group, head_dim), jnp.float32),
    )
    key_piece = lax.all_gather(keys, "seq", axis=0, tiled=True)
    value_piece = lax.all_gather(values, "seq", axis=0, tiled=True)
    count = key_piece.shape[0]
    blocks = count // KEY_BLOCK
    key_blocks = key_piece.reshape(blocks, KEY_BLOCK, local_kv, head_dim)
    value_blocks = value_piece.reshape(blocks, KEY_BLOCK, local_kv, head_dim)

    def block_step(inner_state, item):
        block_index, key_part, value_part = item
        return (update(inner_state, key_part, value_part, block_index * KEY_BLOCK), None)

    final_state, _ = lax.scan(
        block_step, start_state, (jnp.arange(blocks, dtype=jnp.int32), key_blocks, value_blocks)
    )
    final_max, final_total, final_acc = final_state
    context = (
        (final_acc / final_total[..., None])
        .astype(jnp.bfloat16)
        .reshape(tok_rows, local_heads, head_dim)
    )
    partial_bc = jnp.einsum("tc,jc->tj", inner_x, bc_weight, preferred_element_type=jnp.float32)
    summed_bc = lax.psum(partial_bc, "tp")
    state_size = a_log.shape[0]
    b_rows = summed_bc[:, :state_size]
    c_rows = summed_bc[:, state_size:]
    keep_rows = jnp.where(positions == req_start, 0.0, 1.0).astype(jnp.float32)
    rates = jnp.exp(a_log)
    step_sizes = jax.nn.softplus(dt_raw.astype(jnp.float32) + dt_bias[None, :])
    x_float = inner_x.astype(jnp.float32)

    def local_step(carried, item):
        decay_total, state_now = carried
        step_row, x_row, b_row, keep_row = item
        factor = jnp.exp(-step_row[None, :] * rates) * keep_row
        state_now = factor * state_now + (step_row * x_row)[None, :] * b_row[:, None]
        return ((decay_total * factor, state_now), None)

    ones_state = jnp.ones(rates.shape, jnp.float32)
    zero_state = jnp.zeros(rates.shape, jnp.float32)
    (decay_total, end_state), _ = lax.scan(
        local_step, (ones_state, zero_state), (step_sizes, x_float, b_rows, keep_rows), unroll=8
    )
    incoming = prefix((decay_total, end_state), "seq", chain_combine, (ones_state, zero_state))[1]

    def output_step(state_now, item):
        step_row, x_row, b_row, c_row, keep_row = item
        factor = jnp.exp(-step_row[None, :] * rates) * keep_row
        state_now = factor * state_now + (step_row * x_row)[None, :] * b_row[:, None]
        out_row = jnp.sum(c_row[:, None] * state_now, axis=0) + skip_gain * x_row
        return (state_now, out_row.astype(jnp.bfloat16))

    _, mixed = lax.scan(
        output_step, incoming, (step_sizes, x_float, b_rows, c_rows, keep_rows), unroll=8
    )
    return (steered, context, mixed)


def solution(mesh):
    return jax.shard_map(
        shards,
        mesh=mesh,
        in_specs=(
            P("seq", "tp"),
            P(None, "tp"),
            P(),
            P(),
            P(),
            P("seq", "tp", None),
            P("seq", "tp", None),
            P("seq", "tp", None),
            P("seq", "tp"),
            P("seq", "tp"),
            P("tp"),
            P(None, "tp"),
            P("tp"),
            P(None, "tp"),
        ),
        out_specs=(P("seq", "tp"), P("seq", "tp", None), P("seq", "tp")),
        check_vma=False,
    )
```

profile of v0, /device:TPU:504, one launch (start us, length us, event | category | flops | bytes accessed | tf_op | source)
XLA Modules:
  0.0 902.7 jit_solution(4664678258861879669)
XLA Ops:
  13.0 25.6 %psum.7 = f32[128,32]{0,1:T(8,128)S(1)} all-reduce(f32[128,32]{0,1:T(8,128)S(1)} %fusion.102), channel_id=1, replica_groups=mesh['seq'=64,'tp'=8] {'tp'}, use_global_device_ids=true, to_apply=%region_6.7 | all-reduce | flops 4096 | bytes 32768 | tf_op jit(solution)/shard_map/psum | solution.py:123
  39.4 180.9 %while.55 = (s32[]{:T(128)}, f32[16,2048]{1,0:T(8,128)S(1)}, f32[16,2048]{1,0:T(8,128)S(1)}, f32[16,8,2048]{2,1,0:T(8,128)S(1)}, f32[16,2048]{1,0:T(8,128)S(1)},...) while((s32[]{:T(128)}, f32[16,2048]{1,0:T(8,128)S(1)}, ...), condition=%wide.region_8.9_spmd.clone, body=%wide.region_7.8_spmd.clone.sunk | while | flops 2195466 | bytes 1248228 | solution.py:141
  40.3 5.3 fusion.130
  45.6 5.2 fusion.129
  51.6 5.3 fusion.130
  56.9 5.2 fusion.129
  62.9 5.3 fusion.130
  68.2 5.2 fusion.129
  74.2 5.3 fusion.130
  79.5 5.2 fusion.129
  85.5 5.3 fusion.130
  90.8 5.2 fusion.129
  96.8 5.3 fusion.130
  102.1 5.2 fusion.129
  108.2 5.3 fusion.130
  113.4 5.2 fusion.129
  119.5 5.3 fusion.130
  124.7 5.2 fusion.129
  130.8 5.3 fusion.130
  136.0 5.2 fusion.129
  142.1 5.3 fusion.130
  147.3 5.2 fusion.129
  153.4 5.3 fusion.130
  158.6 5.2 fusion.129
  164.7 5.3 fusion.130
  169.9 5.2 fusion.129
  176.0 5.3 fusion.130
  181.3 5.2 fusion.129
  187.3 5.3 fusion.130
  192.6 5.2 fusion.129
  198.6 5.3 fusion.130
  203.9 5.2 fusion.129
  209.9 5.3 fusion.130
  215.2 5.2 fusion.129
  224.0 2.1 fusion.87
  226.1 61.9 %all-gather.9.cloned.1.call-done = bf16[8192,1,128]{2,0,1:T(8,128)(2,1)} async-done(((bf16[128,1,128]{2,0,1:T(8,128)(2,1)}), bf16[8192,1,128]{2,0,1:T(8,128)(2,1)}) %all-gather.9.cloned.1.call-update) | async-done | bytes 2097168 | tf_op jit(solution)/shard_map/all_gather | solution.py:103
  288.1 78.5 %while.54 = (s32[]{:T(128)}, f32[128,1,8]{0,2,1:T(8,128)S(1)}, f32[128,1,8]{0,2,1:T(8,128)S(1)}, f32[128,1,8,128]{0,3,2,1:T(8,128)S(1)}, s32[16]{0:T(128)S(1)}, ...) while((s32[]{:T(128)}, f32[128,1,8]{0,2,1:T(8,128)S(1)}, ...), condition=%wide.region_5.6_spmd.clone, body=%wide.region_2.5_spmd.clone.sunk | while | flops 275847808 | bytes 8198825 | solution.py:113
  367.8 74.9 %all-gather.11.cloned.1.call-done = f32[1024,2048]{1,0:T(8,128)} async-done(((f32[16,2048]{1,0:T(8,128)}), f32[1024,2048]{1,0:T(8,128)}) %all-gather.11.cloned.1.call-update) | async-done | bytes 8388624 | tf_op jit(solution)/shard_map/all_gather | solution.py:12
  442.7 153.9 %all-gather.13.cloned.1.call-done = f32[1024,2048]{1,0:T(8,128)} async-done(((f32[16,2048]{1,0:T(8,128)}), f32[1024,2048]{1,0:T(8,128)}) %all-gather.13.cloned.1.call-update) | async-done | bytes 8388624 | tf_op jit(solution)/shard_map/all_gather | solution.py:12
  596.6 67.0 %while.52 = (s32[]{:T(128)}, f32[16,2048]{1,0:T(8,128)S(1)}, s32[]{:T(128)}, f32[64,16,2048]{2,1,0:T(8,128)}, f32[64,16,2048]{2,1,0:T(8,128)}, /*index=5*/s32[]{:T(128)}, s32[]{:T(128)}, s32[]{:T(128)}) while((s32[]{:T(128)}, f32[16,2048]{1,0:T(8,128)S(1)}, s32[]{:T(128)}, f32[64,16,2048]{2,1,0:T(8,128)}, f32[64,16,2048]{2,1,0:T(8,128)}, ...), condition=%wide.region_10.11_spmd, body=%wide.region_9.10_spmd.sunk | while | flops 65541 | bytes 524411 | solution.py:20
  663.6 232.7 %while.53 = (s32[]{:T(128)}, f32[16,2048]{1,0:T(8,128)S(1)}, bf16[16,8,2048]{2,1,0:T(8,128)(2,1)}, f32[16,8,2048]{2,1,0:T(8,128)}, f32[16,2048]{1,0:T(8,128)S(1)...) while((s32[]{:T(128)}, f32[16,2048]{1,0:T(8,128)S(1)}, ...), condition=%wide.region_20.21_spmd, body=%wide.region_11.20_spmd.sunk | while | flops 2883593 | bytes 1915265 | solution.py:153
  666.9 2.0 multiply_reduce_fusion.13
  668.9 5.1 multiply_reduce_fusion.11
  681.1 2.0 multiply_reduce_fusion.13
  683.1 5.1 multiply_reduce_fusion.11
  695.7 2.0 multiply_reduce_fusion.13
  697.7 5.1 multiply_reduce_fusion.11
  712.5 5.1 multiply_reduce_fusion.11
  724.7 2.0 multiply_reduce_fusion.13
  726.7 5.1 multiply_reduce_fusion.11
  741.0 5.1 multiply_reduce_fusion.11
  755.5 5.1 multiply_reduce_fusion.11
  765.0 2.2 fusion.119
  768.6 2.0 multiply_reduce_fusion.13
  770.6 5.1 multiply_reduce_fusion.11
  785.1 5.1 multiply_reduce_fusion.11
  797.7 2.0 multiply_reduce_fusion.13
  799.7 5.1 multiply_reduce_fusion.11
  814.2 5.1 multiply_reduce_fusion.11
  828.7 5.1 multiply_reduce_fusion.11
  843.1 5.1 multiply_reduce_fusion.11
  857.9 5.1 multiply_reduce_fusion.11
  872.4 5.1 multiply_reduce_fusion.11
  887.0 5.1 multiply_reduce_fusion.11
  (533 shorter events, 294.1 us)
Async XLA Ops:
  7.2 4.5 copy-start
  7.2 31.6 %copy-start.8 = (f32[16,2048]{1,0:T(8,128)S(1)}, f32[16,2048]{1,0:T(8,128)}, u32[]{:S(2)}) copy-start(f32[16,2048]{1,0:T(8,128)} %param.33) | copy-start | bytes 393220
  7.2 31.6 %copy-start.4 = (bf16[128,2048]{1,0:T(8,128)(2,1)S(1)}, bf16[128,2048]{1,0:T(8,128)(2,1)}, u32[]{:S(2)}) copy-start(bf16[128,2048]{1,0:T(8,128)(2,1)} %param.31) | copy-start | bytes 1572868
  7.2 31.6 %copy-start.10 = (f32[2048]{0:T(1024)S(1)}, f32[2048]{0:T(1024)}, u32[]{:S(2)}) copy-start(f32[2048]{0:T(1024)} %param.32) | copy-start | bytes 24580
  7.2 218.9 %all-gather.7.cloned.1.call-start = ((), (), s32[]{:S(2)}) async-start(), calls=%async_computation | async-start | bytes 2129920 | tf_op jit(solution)/shard_map/all_gather | solution.py:102
  7.9 280.1 %all-gather.9.cloned.1.call-start = ((), (), s32[]{:S(2)}) async-start(), calls=%async_computation.1 | async-start | bytes 2129920 | tf_op jit(solution)/shard_map/all_gather | solution.py:103
  8.7 434.0 %all-gather.11.cloned.1.call-start = ((), (), s32[]{:S(2)}) async-start(), calls=%async_computation.2 | async-start | bytes 8519680 | tf_op jit(solution)/shard_map/all_gather | solution.py:12
  10.3 2.7 copy-start.11
  39.4 183.0 %copy-start.5 = (bf16[128,8,128]{2,1,0:T(8,128)(2,1)S(1)}, bf16[128,8,128]{2,1,0:T(8,128)(2,1)}, u32[]{:S(2)}) copy-start(bf16[128,8,128]{2,1,0:T(8,128)(2,1)} %param.27) | copy-start | bytes 786436
  220.3 0.7 copy-start.9
  220.4 0.7 copy-start.1
  220.4 1.3 copy-start.7
  220.4 67.7 %copy-start.2 = (f32[16,8,2048]{2,1,0:T(8,128)}, f32[16,8,2048]{2,1,0:T(8,128)S(1)}, u32[]{:S(2)}) copy-start(f32[16,8,2048]{2,1,0:T(8,128)S(1)} %get-tuple-element.1075) | copy-start | bytes 3145732
  220.4 67.7 %copy-start.3 = (f32[16,8,2048]{2,1,0:T(8,128)}, f32[16,8,2048]{2,1,0:T(8,128)S(1)}, u32[]{:S(2)}) copy-start(f32[16,8,2048]{2,1,0:T(8,128)S(1)} %get-tuple-element.1076) | copy-start | bytes 3145732
  221.0 375.5 %all-gather.13.cloned.1.call-start = ((), (), s32[]{:S(2)}) async-start(), calls=%async_computation.3 | async-start | bytes 8519680 | tf_op jit(solution)/shard_map/all_gather | solution.py:12
  366.8 296.7 %copy-start.6 = (f32[2048]{0:T(1024)S(1)}, f32[2048]{0:T(1024)}, u32[]{:S(2)}) copy-start(f32[2048]{0:T(1024)} %param.34) | copy-start | bytes 24580
Sparse Core Ops, SparseCore 0:
  11.0 137.2 all-gather.6
  151.2 136.8 all-gather.8
  291.0 151.6 all-gather.10
  445.5 151.0 all-gather.12
where the time goes:
time: 912 us; the launch traced here: 903 us
  other arithmetic  449 us (49%)
  waiting for transfers between devices  293 us (32%)
  local copies, waits for them, and re-layouts  56.6 us (6%)
  matrix products  52.2 us (6%)
  blocking collectives  25.6 us (3%)
  between operations  14.1 us (2%)
  loops' own time  12.7 us (1%)
    all_gather x2, waiting for transfers between devices, prefix(): gathered = jax.tree.map(lambda a: lax.all_gather(a, axis), part)  229 us
    reduce_sum x48, other arithmetic, output_step(): out_row = jnp.sum(c_row[:, None] * state_now, axis=0) + skip_gain * x_row  147 us
    add x16, other arithmetic, local_step(): factor * state_now + (step_row * x_row)[None, :] * b_row[:, None]  84.3 us
    mul x16, other arithmetic, local_step(): return ((decay_total * factor, state_now), None)  82.6 us
    add x63, other arithmetic, chain_combine(): return (earlier[0] * later[0], later[0] * earlier[1] + later[1])  65.4 us
    all_gather x1, waiting for transfers between devices, shards(): value_piece = lax.all_gather(values, 'seq', axis=0, tiled=True)  61.9 us
    mul x16, other arithmetic, output_step(): step_row * x_row  29.2 us
    dot_general x16, matrix products, update(): jnp.einsum('tkgs,skd->tkgd', weights, value_part, preferred_element_type=...  26 us
  transfers between devices with their start and end apart: 4, of which 3 were waited for; matrix products, arithmetic and copies ran while one was open for 29% of the time, Pallas kernels for 0%

commit v1 on v0

--- a/solution.py
+++ b/solution.py
@@ -120,7 +120,7 @@
         .reshape(tok_rows, local_heads, head_dim)
     )
     partial_bc = jnp.einsum("tc,jc->tj", inner_x, bc_weight, preferred_element_type=jnp.float32)
-    summed_bc = lax.psum(partial_bc, "tp")
+    summed_bc = jnp.sum(lax.all_gather(partial_bc, "tp"), axis=0)
     state_size = a_log.shape[0]
     b_rows = summed_bc[:, :state_size]
     c_rows = summed_bc[:, state_size:]

time: 912 us -> 912 us (level)
  blocking collectives: 25.6 us -> 13.1 us
  waiting for transfers between devices: 293 us -> 305 us
    psum x1 -> x0, blocking collectives: 25.6 us -> none  [shards(): summed_bc = lax.psum(partial_bc, 'tp')]
    all_gather x0 -> x1, blocking collectives: none -> 13.1 us  [shards(): summed_bc = jnp.sum(lax.all_gather(partial_bc, 'tp'), axis=0)]
    all_gather x1, waiting for transfers between devices: 61.9 us -> 74.4 us  [shards(): value_piece = lax.all_gather(values, 'seq', axis=0, tiled=True)]
where the time goes in v1:
time: 912 us; the launch traced here: 903 us
  other arithmetic  449 us (49%)
  waiting for transfers between devices  305 us (33%)
  local copies, waits for them, and re-layouts  56.6 us (6%)
  matrix products  52.2 us (6%)
  between operations  14.1 us (2%)
  blocking collectives  13.1 us (1%)
  loops' own time  12.7 us (1%)
    all_gather x2, waiting for transfers between devices, prefix(): gathered = jax.tree.map(lambda a: lax.all_gather(a, axis), part)  229 us
    reduce_sum x48, other arithmetic, output_step(): out_row = jnp.sum(c_row[:, None] * state_now, axis=0) + skip_gain * x_row  147 us
    add x16, other arithmetic, local_step(): factor * state_now + (step_row * x_row)[None, :] * b_row[:, None]  84.3 us
    mul x16, other arithmetic, local_step(): return ((decay_total * factor, state_now), None)  82.6 us
    all_gather x1, waiting for transfers between devices, shards(): value_piece = lax.all_gather(values, 'seq', axis=0, tiled=True)  74.4 us
    add x63, other arithmetic, chain_combine(): return (earlier[0] * later[0], later[0] * earlier[1] + later[1])  65.3 us
    mul x16, other arithmetic, output_step(): step_row * x_row  29.2 us
    dot_general x16, matrix products, update(): jnp.einsum('tkgs,skd->tkgd', weights, value_part, preferred_element_type=...  26 us
  transfers between devices with their start and end apart: 4, of which 3 were waited for; matrix products, arithmetic and copies ran while one was open for 29% of the time, Pallas kernels for 0%

profile of v1, /device:TPU:504, one launch (start us, length us, event | category | flops | bytes accessed | tf_op | source)
XLA Modules:
  0.0 902.7 jit_solution(5922571319332164940)
XLA Ops:
  13.0 13.1 %all-gather = f32[1024,32]{0,1:T(8,128)S(1)} all-gather(f32[128,32]{0,1:T(8,128)S(1)} %fusion.102), channel_id=2, replica_groups=mesh['seq'=64,'tp'=8] {'tp'}, dimensions={0}, use_global_device_ids=true | all-gather | bytes 147456 | tf_op jit(solution)/shard_map/all_gather | solution.py:123
  27.0 180.9 %while.55 = (s32[]{:T(128)}, f32[16,2048]{1,0:T(8,128)S(1)}, f32[16,2048]{1,0:T(8,128)S(1)}, f32[16,8,2048]{2,1,0:T(8,128)S(1)}, f32[16,2048]{1,0:T(8,128)S(1)},...) while((s32[]{:T(128)}, f32[16,2048]{1,0:T(8,128)S(1)}, ...), condition=%wide.region_8.9_spmd.clone, body=%wide.region_7.8_spmd.clone.sunk | while | flops 2195466 | bytes 1248228 | solution.py:141
  27.9 5.3 fusion.130
  33.2 5.2 fusion.129
  39.2 5.3 fusion.130
  44.5 5.2 fusion.129
  50.5 5.3 fusion.130
  55.8 5.2 fusion.129
  61.8 5.3 fusion.130
  67.1 5.2 fusion.129
  73.1 5.3 fusion.130
  78.4 5.2 fusion.129
  84.4 5.3 fusion.130
  89.7 5.2 fusion.129
  95.7 5.3 fusion.130
  101.0 5.2 fusion.129
  107.0 5.3 fusion.130
  112.3 5.2 fusion.129
  118.3 5.3 fusion.130
  123.6 5.2 fusion.129
  129.6 5.3 fusion.130
  134.9 5.2 fusion.129
  141.0 5.3 fusion.130
  146.2 5.2 fusion.129
  152.3 5.3 fusion.130
  157.5 5.2 fusion.129
  163.6 5.3 fusion.130
  168.8 5.2 fusion.129
  174.9 5.3 fusion.130
  180.1 5.2 fusion.129
  186.2 5.3 fusion.130
  191.4 5.2 fusion.129
  197.5 5.3 fusion.130
  202.8 5.2 fusion.129
  211.6 2.1 fusion.87
  213.7 74.4 %all-gather.10.cloned.1.call-done = bf16[8192,1,128]{2,0,1:T(8,128)(2,1)} async-done(((bf16[128,1,128]{2,0,1:T(8,128)(2,1)}), bf16[8192,1,128]{2,0,1:T(8,128)(2,1)}) %all-gather.10.cloned.1.call-update) | async-done | bytes 2097168 | tf_op jit(solution)/shard_map/all_gather | solution.py:103
  288.1 78.5 %while.54 = (s32[]{:T(128)}, f32[128,1,8]{0,2,1:T(8,128)S(1)}, f32[128,1,8]{0,2,1:T(8,128)S(1)}, f32[128,1,8,128]{0,3,2,1:T(8,128)S(1)}, s32[16]{0:T(128)S(1)}, ...) while((s32[]{:T(128)}, f32[128,1,8]{0,2,1:T(8,128)S(1)}, ...), condition=%wide.region_5.6_spmd.clone, body=%wide.region_2.5_spmd.clone.sunk | while | flops 275847808 | bytes 8198825 | solution.py:113
  367.8 74.9 %all-gather.12.cloned.1.call-done = f32[1024,2048]{1,0:T(8,128)} async-done(((f32[16,2048]{1,0:T(8,128)}), f32[1024,2048]{1,0:T(8,128)}) %all-gather.12.cloned.1.call-update) | async-done | bytes 8388624 | tf_op jit(solution)/shard_map/all_gather | solution.py:12
  442.7 153.9 %all-gather.14.cloned.1.call-done = f32[1024,2048]{1,0:T(8,128)} async-done(((f32[16,2048]{1,0:T(8,128)}), f32[1024,2048]{1,0:T(8,128)}) %all-gather.14.cloned.1.call-update) | async-done | bytes 8388624 | tf_op jit(solution)/shard_map/all_gather | solution.py:12
  596.6 66.9 %while.52 = (s32[]{:T(128)}, f32[16,2048]{1,0:T(8,128)S(1)}, s32[]{:T(128)}, f32[64,16,2048]{2,1,0:T(8,128)}, f32[64,16,2048]{2,1,0:T(8,128)}, /*index=5*/s32[]{:T(128)}, s32[]{:T(128)}, s32[]{:T(128)}) while((s32[]{:T(128)}, f32[16,2048]{1,0:T(8,128)S(1)}, s32[]{:T(128)}, f32[64,16,2048]{2,1,0:T(8,128)}, f32[64,16,2048]{2,1,0:T(8,128)}, ...), condition=%wide.region_10.11_spmd, body=%wide.region_9.10_spmd.sunk | while | flops 65541 | bytes 524411 | solution.py:20
  663.5 232.7 %while.53 = (s32[]{:T(128)}, f32[16,2048]{1,0:T(8,128)S(1)}, bf16[16,8,2048]{2,1,0:T(8,128)(2,1)}, f32[16,8,2048]{2,1,0:T(8,128)}, f32[16,2048]{1,0:T(8,128)S(1)...) while((s32[]{:T(128)}, f32[16,2048]{1,0:T(8,128)S(1)}, ...), condition=%wide.region_20.21_spmd, body=%wide.region_11.20_spmd.sunk | while | flops 2883593 | bytes 1915265 | solution.py:153
  668.8 5.1 multiply_reduce_fusion.11
  681.1 2.0 multiply_reduce_fusion.13
  683.1 5.1 multiply_reduce_fusion.11
  695.6 2.0 multiply_reduce_fusion.13
  697.6 5.1 multiply_reduce_fusion.11
  710.4 2.0 multiply_reduce_fusion.13
  712.4 5.1 multiply_reduce_fusion.11
  724.7 2.0 multiply_reduce_fusion.13
  726.7 5.1 multiply_reduce_fusion.11
  738.9 2.0 multiply_reduce_fusion.13
  740.9 5.1 multiply_reduce_fusion.11
  755.5 5.1 multiply_reduce_fusion.11
  765.0 2.2 fusion.119
  768.5 2.0 multiply_reduce_fusion.13
  770.6 5.1 multiply_reduce_fusion.11
  785.1 5.1 multiply_reduce_fusion.11
  799.7 5.1 multiply_reduce_fusion.11
  814.1 5.1 multiply_reduce_fusion.11
  828.7 5.1 multiply_reduce_fusion.11
  843.1 5.1 multiply_reduce_fusion.11
  857.9 5.1 multiply_reduce_fusion.11
  872.4 5.1 multiply_reduce_fusion.11
  886.9 5.1 multiply_reduce_fusion.11
  (535 shorter events, 294.1 us)
Async XLA Ops:
  7.2 4.5 copy-start
  7.2 19.1 %copy-start.8 = (f32[16,2048]{1,0:T(8,128)S(1)}, f32[16,2048]{1,0:T(8,128)}, u32[]{:S(2)}) copy-start(f32[16,2048]{1,0:T(8,128)} %param.33) | copy-start | bytes 393220
  7.2 19.2 %copy-start.4 = (bf16[128,2048]{1,0:T(8,128)(2,1)S(1)}, bf16[128,2048]{1,0:T(8,128)(2,1)}, u32[]{:S(2)}) copy-start(bf16[128,2048]{1,0:T(8,128)(2,1)} %param.31) | copy-start | bytes 1572868
  7.2 19.2 %copy-start.10 = (f32[2048]{0:T(1024)S(1)}, f32[2048]{0:T(1024)}, u32[]{:S(2)}) copy-start(f32[2048]{0:T(1024)} %param.32) | copy-start | bytes 24580
  7.2 206.5 %all-gather.8.cloned.1.call-start = ((), (), s32[]{:S(2)}) async-start(), calls=%async_computation | async-start | bytes 2129920 | tf_op jit(solution)/shard_map/all_gather | solution.py:102
  7.9 280.1 %all-gather.10.cloned.1.call-start = ((), (), s32[]{:S(2)}) async-start(), calls=%async_computation.1 | async-start | bytes 2129920 | tf_op jit(solution)/shard_map/all_gather | solution.py:103
  8.7 434.0 %all-gather.12.cloned.1.call-start = ((), (), s32[]{:S(2)}) async-start(), calls=%async_computation.2 | async-start | bytes 8519680 | tf_op jit(solution)/shard_map/all_gather | solution.py:12
  10.3 15.9 %copy-start.11 = (s32[4]{0:T(128)}, s32[4]{0:T(128)S(1)}, u32[]{:S(2)}) copy-start(s32[4]{0:T(128)S(1)} %bitcast_subtract_fusion) | copy-start | bytes 52
  27.0 183.0 %copy-start.5 = (bf16[128,8,128]{2,1,0:T(8,128)(2,1)S(1)}, bf16[128,8,128]{2,1,0:T(8,128)(2,1)}, u32[]{:S(2)}) copy-start(bf16[128,8,128]{2,1,0:T(8,128)(2,1)} %param.27) | copy-start | bytes 786436
  207.9 0.7 copy-start.9
  207.9 0.7 copy-start.1
  207.9 1.3 copy-start.7
  208.0 80.1 %copy-start.2 = (f32[16,8,2048]{2,1,0:T(8,128)}, f32[16,8,2048]{2,1,0:T(8,128)S(1)}, u32[]{:S(2)}) copy-start(f32[16,8,2048]{2,1,0:T(8,128)S(1)} %get-tuple-element.1131) | copy-start | bytes 3145732
  208.0 80.1 %copy-start.3 = (f32[16,8,2048]{2,1,0:T(8,128)}, f32[16,8,2048]{2,1,0:T(8,128)S(1)}, u32[]{:S(2)}) copy-start(f32[16,8,2048]{2,1,0:T(8,128)S(1)} %get-tuple-element.1132) | copy-start | bytes 3145732
  208.6 388.0 %all-gather.14.cloned.1.call-start = ((), (), s32[]{:S(2)}) async-start(), calls=%async_computation.3 | async-start | bytes 8519680 | tf_op jit(solution)/shard_map/all_gather | solution.py:12
  366.8 296.7 %copy-start.6 = (f32[2048]{0:T(1024)S(1)}, f32[2048]{0:T(1024)}, u32[]{:S(2)}) copy-start(f32[2048]{0:T(1024)} %param.34) | copy-start | bytes 24580
Sparse Core Ops, SparseCore 0:
  11.0 137.1 all-gather.7
  151.1 136.9 all-gather.9
  291.0 151.6 all-gather.11
  445.5 151.0 all-gather.13
